TPU v7x, 128 devices: a whole 4x4x4 slice. The times are simulated.
128 devices in a mesh: lag: 8 (over y, x_lo), row: 16 (over x_hi, z, core).
Axes of the slice: x: 4 (x_hi: 2, x_lo: 2; x = x_hi * 2 + x_lo), y: 4, z: 4, core: 2. Of those that a mesh axis runs over, the one named last changes fastest.
Arguments:
- lag_weights: float32 [32, 4096, 4096], P('lag', 'row'), may hold values from -0.015625 to 0.015625
- inverse_head: float32 [4096, 4096], P('row'), may hold values from -0.09375 to 0.09375
- excitation: float32 [3, 4096, 128], P(None, 'row'), may hold values from -6 to 6
- history: float32 [32, 4096, 128], P('lag', 'row'), may hold values from -6 to 6
Outputs:
- densities: float32 [3, 4096, 128], P(None, 'row')
All inputs are finite; a program needn't handle non-finite values.
Results may differ from a plain program's by a relative error of at most 0.0001.
Values sent between devices are 32-bit elements; how exact they have to be, the bound alone decides.
A program may use at most 128 MiB of HBM per device.

v0:
```python
import jax
import jax.numpy as jnp
from jax import lax
from jax.sharding import PartitionSpec as P

STEPS = 3


def sent_to_all(shard, axis):
    devices = lax.axis_size(axis)
    return lax.all_to_all(
        jnp.broadcast_to(shard[None], (devices, *shard.shape)), axis, 0, 0, tiled=True
    )


def over_copies(shard, axis):
    return sent_to_all(shard, axis).sum(axis=0)


def in_order(pieces, dim):
    dims = list(pieces.shape[1:])
    dims[dim] *= pieces.shape[0]
    return jnp.moveaxis(pieces, 0, dim).reshape(dims)


def gathered_copies(shard, axis, dim):
    return in_order(sent_to_all(shard, axis), dim)


def from_behind(value, axis, steps):
    count = lax.axis_size(axis)
    leading, last = (max(0, -steps), min(count, count - steps))
    return lax.ppermute(value, axis, [(source, source + steps) for source in range(leading, last)])


def lag_products(weights, piece):
    return jnp.einsum("kmc,kcr->mr", weights, piece, precision=lax.Precision.HIGHEST)


def on_device(lag_weights, inverse_head, excitation, history):
    at_head = lax.axis_index("lag") == 0
    past = lax.all_gather(history, "row", axis=1, tiled=True)
    results = []
    for step in range(STEPS):
        carried = lag_products(lag_weights, past)
        carried = over_copies(carried, "lag")
        right_side = excitation[step] - carried
        density = jnp.dot(
            inverse_head,
            gathered_copies(right_side, "row", 0),
            precision=lax.Precision.HIGHEST,
            preferred_element_type=jnp.float32,
        )
        results.append(density)
        if step + 1 < STEPS:
            whole_density = lax.all_gather(density, "row", axis=0, tiled=True)
            moved = from_behind(past[-1], "lag", 1)
            entering = jnp.where(at_head, whole_density, moved)
            past = jnp.concatenate([entering[None], past[:-1]], axis=0)
    return jnp.stack(results, axis=0)


def solution(mesh):
    placed = (P("lag", "row", None), P("row", None), P(None, "row", None), P("lag", "row", None))
    return jax.shard_map(
        on_device, mesh=mesh, in_specs=placed, out_specs=P(None, "row", None), check_vma=False
    )
```

profile of v0, /device:TPU:1, one launch (start us, length us, event | category | flops | bytes accessed | tf_op | source)
XLA Modules:
  0.0 446.9 jit_solution(8277773772511604061)
XLA Ops:
  6.5 0.7 all-gather.4.cloned.1.call-update
  7.3 79.4 %all-gather.4.cloned.1.call-done = f32[4,4096,128]{2,1,0:T(8,128)} async-done(((f32[4,256,128]{2,1,0:T(8,128)}), f32[4,4096,128]{2,1,0:T(8,128)}) %all-gather.4.cloned.1.call-update) | async-done | bytes 8388624 | tf_op jit(solution)/shard_map/all_gather | solution.py:42
  86.7 16.8 %convolution_bitcast_fusion.1 = f32[256,128]{1,0:T(8,128)S(1)} fusion(f32[4,256,4096]{2,1,0:T(8,128)} %param.4, f32[4,4096,128]{2,1,0:T(8,128)} %all-gather.4.cloned.1.call-done), kind=kOutput, calls=%fused_computation.16 | convolution fusion | flops 6442450944 | bytes 25296896 | tf_op jit(solution)/shard_map/kmc,kcr->mr/dot_general | solution.py:37
  103.5 18.8 %all_to_all.30 = f32[8,256,128]{2,1,0:T(8,128)S(1)} all-to-all(f32[8,256,128]{2,1,0:T(8,128)S(1)} %broadcast_in_dim.22), channel_id=1, replica_groups=mesh['lag'=8,'row'=16] {'lag'}, dimensions={0} | all-to-all | bytes 2097152 | tf_op jit(solution)/shard_map/all_to_all | solution.py:11
  122.4 1.1 fusion.17
  123.5 0.2 broadcast_in_dim.24
  123.7 33.9 %all_to_all.31 = f32[16,256,128]{2,1,0:T(8,128)S(1)} all-to-all(f32[16,256,128]{2,1,0:T(8,128)S(1)} %broadcast_in_dim.24), channel_id=1, replica_groups=mesh['lag'=8,'row'=16] {'row'}, dimensions={0} | all-to-all | bytes 4194304 | tf_op jit(solution)/shard_map/all_to_all | solution.py:11
  157.6 4.1 fusion.20
  161.8 4.5 %slice_bitcast_fusion = (f32[4096,128]{1,0:T(8,128)}, f32[4096,128]{1,0:T(8,128)}) fusion(f32[4,4096,128]{2,1,0:T(8,128)} %all-gather.4.cloned.1.call-done), kind=kLoop, calls=%fused_computation.9 | loop fusion | bytes 8388608 | tf_op jit(solution)/shard_map/squeeze | solution.py:57
  166.3 2.2 collective-permute-start
  168.5 5.9 %slice.30 = f32[3,4096,128]{2,1,0:T(8,128)} slice(f32[4,4096,128]{2,1,0:T(8,128)} %all-gather.4.cloned.1.call-done), slice={[0:3], [0:4096], [0:128]} | slice | bytes 12582912 | tf_op jit(solution)/shard_map/slice | solution.py:59
  174.4 44.9 %collective-permute-done = f32[4096,128]{1,0:T(8,128)S(1)} collective-permute-done((f32[4096,128]{1,0:T(8,128)}, f32[4096,128]{1,0:T(8,128)S(1)}, u32[]{:S(2)}, u32[]{:S(2)}) %collective-permute-start) | collective-permute-done | bytes 2097184 | tf_op jit(solution)/shard_map/ppermute | solution.py:33
  219.3 1.3 copy-done.3
  220.7 1.8 select_bitcast_fusion.1
  222.5 21.1 %fusion.9 = f32[256,128]{0,1:T(8,128)S(1)} fusion(f32[4,256,4096]{2,1,0:T(8,128)} %param.4, f32[3,4096,128]{2,1,0:T(8,128)} %slice.30, f32[1,4096,128]{2,1,0:T(8,128)S(1)} %select_bitcast_fusion.1), kind=kOutput, calls=%fused_computation.13 | convolution fusion | flops 6444548096 | bytes 25296896 | tf_op jit(solution)/shard_map/kmc,kcr->mr/dot_general | solution.py:37
  243.6 0.1 copy.14
  243.7 20.4 %all_to_all.32 = f32[8,256,128]{2,1,0:T(8,128)S(1)} all-to-all(f32[8,256,128]{2,1,0:T(8,128)S(1)} %broadcast_in_dim.52), channel_id=1, replica_groups=mesh['lag'=8,'row'=16] {'lag'}, dimensions={0} | all-to-all | bytes 2097152 | tf_op jit(solution)/shard_map/all_to_all | solution.py:11
  264.2 1.1 fusion.16
  265.3 0.2 broadcast_in_dim.54
  265.5 33.5 %all_to_all.33 = f32[16,256,128]{2,1,0:T(8,128)S(1)} all-to-all(f32[16,256,128]{2,1,0:T(8,128)S(1)} %broadcast_in_dim.54), channel_id=1, replica_groups=mesh['lag'=8,'row'=16] {'row'}, dimensions={0} | all-to-all | bytes 4194304 | tf_op jit(solution)/shard_map/all_to_all | solution.py:11
  299.0 4.1 fusion.21
  303.1 4.2 collective-permute-start.1
  307.3 49.4 %collective-permute-done.1 = f32[4096,128]{1,0:T(8,128)} collective-permute-done((f32[4096,128]{1,0:T(8,128)}, f32[4096,128]{1,0:T(8,128)}, u32[]{:S(2)}, u32[]{:S(2)}) %collective-permute-start.1) | collective-permute-done | bytes 2097184 | tf_op jit(solution)/shard_map/ppermute | solution.py:33
  356.7 3.1 select_bitcast_fusion
  359.8 21.1 %fusion.12 = f32[256,128]{0,1:T(8,128)S(1)} fusion(f32[4,256,4096]{2,1,0:T(8,128)} %param.4, f32[3,4096,128]{2,1,0:T(8,128)} %slice.30, f32[1,4096,128]{2,1,0:T(8,128)S(1)} %select_bitcast_fusion.1, f32[1,4096,128]{2,1,0:T(8,128)} %select_bitcast_fusion), kind=kOutput, calls=%fused_computation.15 | convolution fusion | flops 6446645248 | bytes 27394048 | tf_op jit(solution)/shard_map/kmc,kcr->mr/dot_general | solution.py:37
  380.9 0.1 copy.17
  381.1 17.9 %all_to_all.34 = f32[8,256,128]{2,1,0:T(8,128)S(1)} all-to-all(f32[8,256,128]{2,1,0:T(8,128)S(1)} %broadcast_in_dim.56), channel_id=1, replica_groups=mesh['lag'=8,'row'=16] {'lag'}, dimensions={0} | all-to-all | bytes 2097152 | tf_op jit(solution)/shard_map/all_to_all | solution.py:11
  399.0 1.1 fusion.15
  400.1 0.2 broadcast_in_dim.58
  400.3 35.6 %all_to_all.35 = f32[16,256,128]{2,1,0:T(8,128)S(1)} all-to-all(f32[16,256,128]{2,1,0:T(8,128)S(1)} %broadcast_in_dim.58), channel_id=1, replica_groups=mesh['lag'=8,'row'=16] {'row'}, dimensions={0} | all-to-all | bytes 4194304 | tf_op jit(solution)/shard_map/all_to_all | solution.py:11
  435.9 3.4 convolution_bitcast_fusion
  439.4 0.8 pad_maximum_fusion.1
  (24 shorter events, 0.5 us)
Async XLA Ops:
  6.5 80.1 %all-gather.4.cloned.1.call-start = ((), (), s32[]{:S(2)}) async-start(), calls=%async_computation.6 | async-start | bytes 8912896 | tf_op jit(solution)/shard_map/all_gather | solution.py:42
  7.3 213.4 %all-gather.6.cloned.1.call-start = ((), (), s32[]{:S(2)}) async-start(), calls=%async_computation.7 | async-start | bytes 2228224 | tf_op jit(solution)/shard_map/all_gather | solution.py:56
  122.4 35.2 %copy-start = (f32[256,4096]{1,0:T(8,128)S(1)}, f32[256,4096]{1,0:T(8,128)}, u32[]{:S(2)}) copy-start(f32[256,4096]{1,0:T(8,128)} %param.5) | copy-start | bytes 12582916
  161.7 194.9 %all-gather.8.cloned.1.call-start = ((), (), s32[]{:S(2)}) async-start(), calls=%async_computation.8 | async-start | bytes 2228224 | tf_op jit(solution)/shard_map/all_gather | solution.py:56
  166.3 53.0 %collective-permute-start = (f32[4096,128]{1,0:T(8,128)}, f32[4096,128]{1,0:T(8,128)S(1)}, u32[]{:S(2)}, u32[]{:S(2)}) collective-permute-start(f32[4096,128]{1,0:T(8,128)} %get-tuple-element.6), channel_id=1, source_target_pairs={{0,16},{16,32},{32,48},{48,64},{64,80},{80,96},{96,112},{1,17},{17... | collective-permute-start | bytes 6291464 | tf_op jit(solution)/shard_map/ppermute | solution.py:33
  219.3 1.3 copy-start.3
  264.2 34.8 %copy-start.1 = (f32[256,4096]{1,0:T(8,128)S(1)}, f32[256,4096]{1,0:T(8,128)}, u32[]{:S(2)}) copy-start(f32[256,4096]{1,0:T(8,128)} %param.5) | copy-start | bytes 12582916
  303.1 53.5 %collective-permute-start.1 = (f32[4096,128]{1,0:T(8,128)}, f32[4096,128]{1,0:T(8,128)}, u32[]{:S(2)}, u32[]{:S(2)}) collective-permute-start(f32[4096,128]{1,0:T(8,128)} %get-tuple-element.5), channel_id=1, source_target_pairs={{0,16},{16,32},{32,48},{48,64},{64,80},{80,96},{96,112},{1,17},{17... | collective-permute-start | bytes 6291464 | tf_op jit(solution)/shard_map/ppermute | solution.py:33
  399.0 36.9 %copy-start.2 = (f32[256,4096]{1,0:T(8,128)S(1)}, f32[256,4096]{1,0:T(8,128)}, u32[]{:S(2)}) copy-start(f32[256,4096]{1,0:T(8,128)} %param.5) | copy-start | bytes 12582916
  435.9 3.5 copy-start.4
  435.9 3.5 copy-start.5
Sparse Core Ops, SparseCore 0:
  9.9 76.7 all-gather.3
  161.9 49.8 all-gather.5
  303.3 50.0 all-gather.7
where the time goes:
time: 454 us; the launch traced here: 447 us
  waiting for transfers between devices  174 us (38%)
  blocking collectives  160 us (35%)
  matrix products  70.6 us (16%)
  between operations  13.5 us (3%)
  local copies, waits for them, and re-layouts  12.7 us (3%)
  other arithmetic  9.11 us (2%)
  starting transfers between devices  6.42 us (1%)
    all_to_all x6, blocking collectives, sent_to_all(): lax.all_to_all(jnp.broadcast_to(shard[None], (devices, *shard.shape)), ax...  160 us
    ppermute x2, waiting for transfers between devices, from_behind(): lax.ppermute(value, axis, [(source, source + steps) for source in range(l...  94.3 us
    all_gather x1, waiting for transfers between devices, on_device(): past = lax.all_gather(history, 'row', axis=1, tiled=True)  79.4 us
    dot_general x3, matrix products, lag_products(): jnp.einsum('kmc,kcr->mr', weights, piece, precision=lax.Precision.HIGHEST)  58.9 us
    dot_general x3, matrix products, on_device(): jnp.dot(inverse_head, gathered_copies(right_side, 'row', 0), precision=la...  11.7 us
  transfers between devices with their start and end apart: 5, of which 3 were waited for; matrix products, arithmetic and copies ran while one was open for 2% of the time, Pallas kernels for 0%

commit v1 on v0

v1 whole, which is shorter than its diff:
```python
import jax
import jax.numpy as jnp
from jax import lax
from jax.experimental import pallas as pl
from jax.experimental.pallas import tpu as pltpu
from jax.sharding import PartitionSpec as P

STEPS = 3
LAGS = 4
ROWS = 256
M = 4096
EXC = 128
BLOCK = 512
F32 = jnp.float32
BF16 = jnp.bfloat16
MESH = pl.DeviceIdType.MESH
NT = (((1,), (1,)), ((), ()))
NEAR = ((0, 0), (0, 1), (0, 3), (1, 0), (0, 2), (1, 1), (1, 3), (1, 2))


def halves(value):
    high = value.astype(BF16)
    return high, (value - high.astype(F32)).astype(BF16)


def kernel(
    w_hbm, h_hbm, x_hbm, p_hbm, out_ref,
    wv, pg, h_own, h_sib, ht_hi, ht_lo, w12, xv, acc,
    ct, hb, ub, rb, ab, db, mb, ob, sb,
    local_sem, p_send, p_recv, s_send, s_recv, e_send, e_recv, es_send, es_recv,
    w_send, w_recv, in_send, in_recv, c_send, c_recv, r_send, r_recv,
    a_send, a_recv, m_send, m_recv, o_send, o_recv, os_send, os_recv,
):
    lag = lax.axis_index("lag")
    row = lax.axis_index("row")
    chip, core = row // 2, row % 2
    y, x_lo = lag // 2, lag % 2
    x_hi, z = chip // 4, chip % 4

    def near(dx, dz):
        return ((x_hi + dx) % 2) * 4 + (z + dz) % 4

    def at_chip(other):
        return (lag, other * 2 + core)

    def lag_near(k):
        return ((y + k // 2) % 4) * 2 + (x_lo + k % 2) % 2

    def at_lag(other):
        return (other, row)

    sibling = (lag, chip * 2 + 1 - core)

    def rows_of(a_chip, a_core):
        return pl.ds(pl.multiple_of((a_chip * 2 + a_core) * ROWS, ROWS), ROWS)

    def chip_rows(a_chip):
        return pl.ds(pl.multiple_of(a_chip * BLOCK, BLOCK), BLOCK)

    def remote(src, dst, send, recv, device):
        return pltpu.make_async_remote_copy(
            src_ref=src, dst_ref=dst, send_sem=send, recv_sem=recv,
            device_id=device, device_id_type=MESH,
        )

    sends = []

    def go(copy):
        copy.start()
        sends.append(copy)

    mine = rows_of(chip, core)
    locals_ = [
        pltpu.make_async_copy(h_hbm, h_own, local_sem.at[0]),
        pltpu.make_async_copy(p_hbm, pg.at[pl.ds(2, LAGS), mine], local_sem.at[1]),
        pltpu.make_async_copy(x_hbm, xv, local_sem.at[2]),
        pltpu.make_async_copy(w_hbm, wv, local_sem.at[3]),
    ]
    for copy in locals_:
        copy.start()

    barrier = pltpu.get_barrier_semaphore()

    def greet(device):
        pl.semaphore_signal(barrier, inc=1, device_id=device, device_id_type=MESH)

    greet(sibling)
    for k in range(1, 8):
        greet(at_chip(near(k // 4, k % 4)))
        greet(at_lag(lag_near(k)))
    for other in range(8):

        @pl.when(jnp.logical_or(lag != chip, other != lag))
        def _():
            greet((other, lag * 2 + core))

    @pl.when(lag == chip)
    def _():
        pl.semaphore_wait(barrier, 22)

    @pl.when(lag != chip)
    def _():
        pl.semaphore_wait(barrier, 23)

    up, down, across = at_chip(near(0, 1)), at_chip(near(0, 3)), at_chip(near(1, 0))

    class Gather:
        def __init__(self, first, count, send, recv, ssend, srecv):
            self.first, self.count = first, count
            self.send, self.recv, self.ssend, self.srecv = send, recv, ssend, srecv
            half = count // 2
            self.all = (first, count, 0, ROWS)
            self.low = (first, half, 0, ROWS)
            self.high = (first + half, half, 0, ROWS)
            if half == 2:
                self.b1, self.b2 = (first + 2, 1, 0, ROWS), (first + 3, 1, 0, ROWS)
            else:
                self.b1, self.b2 = (first + 1, 1, 0, ROWS // 2), (first + 1, 1, ROWS // 2, ROWS // 2)

        def view(self, dx, dz, part, a_core=None):
            start, count, offset, size = part
            base = (near(dx, dz) * 2 + (core if a_core is None else a_core)) * ROWS + offset
            return pg.at[pl.ds(start, count), pl.ds(pl.multiple_of(base, ROWS // 2), size)]

        def copy(self, index, dx, dz, part, device, src=None):
            view = self.view(dx, dz, part)
            return remote(view if src is None else src, view, self.send.at[index], self.recv.at[index], device)

        def arrived(self, index, dx, dz, part):
            view = self.view(dx, dz, part)
            remote(view, view, self.send.at[index], self.recv.at[index], up).wait_recv()

        def to_sibling(self, index, dx, dz, src=None):
            view = self.view(dx, dz, self.all)
            return remote(view if src is None else src, view, self.ssend.at[index], self.srecv.at[index], sibling)

        def from_sibling(self, index, dx, dz):
            view = self.view(dx, dz, self.all, 1 - core)
            remote(view, view, self.ssend.at[index], self.srecv.at[index], sibling).wait_recv()

        def start(self, src=None):
            return [
                self.copy(0, 0, 0, self.all, up, src),
                self.copy(1, 0, 0, self.all, down, src),
                self.copy(2, 0, 0, self.all, across, src),
                self.to_sibling(0, 0, 0, src),
            ]

        def stage1(self):
            self.arrived(0, 0, 3, self.all)
            out = [self.copy(3, 0, 3, self.low, up), self.copy(5, 0, 3, self.low, across), self.to_sibling(1, 0, 3)]
            yield out
            self.arrived(1, 0, 1, self.all)
            out = [self.copy(4, 0, 1, self.high, down), self.copy(6, 0, 1, self.low, across), self.to_sibling(2, 0, 1)]
            yield out
            self.arrived(2, 1, 0, self.all)
            yield [self.copy(8, 1, 0, self.high, up), self.copy(9, 1, 0, self.high, down), self.to_sibling(3, 1, 0)]

        def stage2(self):
            self.arrived(3, 0, 2, self.low)
            yield [self.copy(7, 0, 2, self.low, across)]
            self.arrived(4, 0, 2, self.high)
            yield [self.to_sibling(4, 0, 2)]
            self.arrived(8, 1, 3, self.high)
            yield [self.copy(10, 1, 3, self.b1, up)]
            self.arrived(9, 1, 1, self.high)
            yield [self.copy(11, 1, 1, self.b2, down)]
            self.arrived(5, 1, 3, self.low)
            yield [self.to_sibling(5, 1, 3)]
            self.arrived(6, 1, 1, self.low)
            yield [self.to_sibling(6, 1, 1)]

        def stage3(self):
            self.arrived(7, 1, 2, self.low)
            self.arrived(10, 1, 2, self.b1)
            self.arrived(11, 1, 2, self.b2)
            yield [self.to_sibling(7, 1, 2)]

        def everything(self):
            return (
                [self.copy(i, 0, 0, self.all, up) for i in range(3)]
                + [self.copy(i, 0, 0, self.low, up) for i in range(3, 10)]
                + [self.copy(i, 0, 0, self.b1, up) for i in (10, 11)]
                + [self.to_sibling(i, 0, 0) for i in range(8)]
            )

    SIB = ((0, 0), (0, 3), (0, 1), (1, 0), (0, 2), (1, 3), (1, 1), (1, 2))
    past = Gather(2, LAGS, p_send, p_recv, s_send, s_recv)
    older = Gather(0, 2, e_send, e_recv, es_send, es_recv)

    for copy in past.start(p_hbm):
        copy.start()
    to_h = remote(h_hbm, h_sib, in_send.at[0], in_recv.at[0], sibling)
    to_h.start()

    e_view = pg.at[pl.ds(0, 2), mine]
    next_group = ((lag + 1) % 8, row)
    handed = remote(p_hbm.at[pl.ds(2, 2)], e_view, in_send.at[1], in_recv.at[1], next_group)

    @pl.when(lag < 7)
    def _():
        handed.start()

    def w_part(n, half):
        return w12.at[n, pl.ds(pl.multiple_of(half * ROWS, ROWS), ROWS)]

    def w_copy(n, k):
        return remote(
            w_hbm.at[n, :, pl.ds(k * BLOCK, BLOCK)], w_part(n, core), w_send.at[n], w_recv.at[n], (k, row)
        )

    def w_keep(n):
        return pltpu.make_async_copy(w_hbm.at[n, :, pl.ds(0, BLOCK)], w_part(n, core), local_sem.at[4 + n])

    @pl.when(lag == 0)
    def _():
        for n in range(2):
            w_keep(n).start()
            for k in range(1, 8):
                w_copy(n, k).start()
        pg[0:2] = jnp.zeros((2, M, EXC), F32)

    def w_sib(n):
        return remote(w_part(n, core), w_part(n, core), w_send.at[2 + n], w_recv.at[2 + n], sibling)

    def w_sib_arrived(n):
        part = w_part(n, 1 - core)
        remote(part, part, w_send.at[2 + n], w_recv.at[2 + n], sibling).wait_recv()

    def w_pass(n):
        @pl.when(lag == 0)
        def _():
            w_keep(n).wait()

        @pl.when(lag != 0)
        def _():
            remote(w_part(n, core), w_part(n, core), w_send.at[n], w_recv.at[n], sibling).wait_recv()

        w_sib(n).start()

    def block_product(n, a_chip):
        rows = chip_rows(a_chip)
        values, highs, lows = [], [], []
        for i in range(LAGS):
            values.append(jnp.concatenate(halves(pg[2 + i - n, rows, :]), axis=1))
            high, low = halves(wv[i, :, rows])
            highs.append(high)
            lows.append(low)
        value = jnp.concatenate(values, axis=0)
        acc[n] += jnp.dot(jnp.concatenate(highs, axis=1), value, preferred_element_type=F32) + jnp.dot(
            jnp.concatenate(lows, axis=1), value, preferred_element_type=F32
        )

    acc[...] = jnp.zeros(acc.shape, F32)

    locals_[0].wait()

    def turn(source, half):
        @pl.loop(0, 8)
        def _(k):
            rows = pl.ds(pl.multiple_of(k * BLOCK, BLOCK), BLOCK)
            lanes = pl.ds(pl.multiple_of(half * ROWS, ROWS), ROWS)
            high, low = halves(source[:, rows].T)
            ht_hi[rows, lanes] = high
            ht_lo[rows, lanes] = low

    turn(h_own, core)
    to_h.wait()
    turn(h_sib, 1 - core)
    locals_[1].wait()
    locals_[3].wait()
    past.from_sibling(0, 0, 0)
    block_product(0, chip)

    for batch in past.stage1():
        for copy in batch:
            copy.start()
    for i in range(1, 4):
        past.from_sibling(i, *SIB[i])
        block_product(0, near(*SIB[i]))
    for batch in past.stage2():
        for copy in batch:
            copy.start()

    @pl.when(lag != 0)
    def _():
        remote(e_view, e_view, in_send.at[1], in_recv.at[1], next_group).wait_recv()
        for copy in older.start():
            copy.start()

    for i in range(4, 7):
        past.from_sibling(i, *SIB[i])
        block_product(0, near(*SIB[i]))
    for batch in past.stage3():
        for copy in batch:
            copy.start()
    locals_[2].wait()
    past.from_sibling(7, *SIB[7])
    block_product(0, near(*SIB[7]))

    @pl.when(lag != 0)
    def _():
        for batch in older.stage1():
            for copy in batch:
                copy.start()

    owner = lax.broadcasted_iota(jnp.int32, (EXC, ROWS), 0) % 64 // 8
    my_half = pl.ds(pl.multiple_of(core * 64, 64), 64)
    other_half = pl.ds(pl.multiple_of((1 - core) * 64, 64), 64)
    my_lanes = pl.ds(pl.multiple_of(core * ROWS, ROWS), ROWS)
    other_lanes = pl.ds(pl.multiple_of((1 - core) * ROWS, ROWS), ROWS)

    def c_copy(n):
        return remote(ct.at[n, other_half], hb.at[n, :, my_lanes], c_send.at[n], c_recv.at[n], sibling)

    def c_arrived(n):
        view = hb.at[n, :, other_lanes]
        remote(view, view, c_send.at[n], c_recv.at[n], sibling).wait_recv()

    def finish_history(n):
        total = (acc[n, :, 0:EXC] + acc[n, :, EXC:]).T
        ct[n] = total - jnp.where(owner == lag, xv[n].T, 0.0)
        c_copy(n).start()
        hb[n, :, my_lanes] = ct[n, my_half]

    def r_start(n):
        for k in range(1, 8):
            other = lag_near(k)
            remote(ub.at[n, other], rb.at[n, k - 1], r_send.at[n], r_recv.at[n], at_lag(other)).start()

    def r_sum(n):
        view = rb.at[n]
        remote(view, view, r_send.at[n], r_recv.at[n], sibling).wait_recv()
        total = ub[n, lag]
        for k in range(7):
            total = total + rb[n, k]
        ab[n, chip] = -total

    def a_start(n):
        for dx, dz in NEAR[1:]:
            k = dx * 4 + dz - 1
            remote(
                ab.at[n, chip], ab.at[n, chip], a_send.at[n], a_recv.at[n, k], at_chip(near(dx, dz))
            ).start()

    def inverse(n):
        total = jnp.zeros((16, BLOCK), F32)
        for dx, dz in NEAR:
            source = near((2 - dx) % 2, (4 - dz) % 4)
            k = dx * 4 + dz - 1
            if k >= 0:
                view = ab.at[n, source]
                remote(view, view, a_send.at[n], a_recv.at[n, k], sibling).wait_recv()
            value = jnp.concatenate(halves(ab[n, source]), axis=0)
            rows = chip_rows(source)
            total = total + jnp.dot(value, ht_hi[rows, :], preferred_element_type=F32)
            total = total + jnp.dot(value, ht_lo[rows, :], preferred_element_type=F32)
        db[n] = total[0:8] + total[8:16]

    def m_copy(n, k):
        other = (chip + k) % 8
        return remote(db.at[n], mb.at[n, lag], m_send.at[n], m_recv.at[n], (chip, other * 2 + core))

    def m_start(n):
        @pl.when(lag != chip)
        def _():
            m_copy(n, 0).start()

        @pl.when(lag == chip)
        def _():
            mb[n, lag] = db[n]

        for k in range(1, 8):
            m_copy(n, k).start()

    def m_wait(n):
        def some(count):
            view = mb.at[n, pl.ds(0, count)]
            copy = remote(view, view, m_send.at[n], m_recv.at[n], sibling)
            copy.wait()

        @pl.when(lag != chip)
        def _():
            some(8)

        @pl.when(lag == chip)
        def _():
            some(7)

    def o_start(n):
        ob[n, lag] = db[n]
        for k in range(1, 8):
            remote(db.at[n], ob.at[n, lag], o_send.at[n], o_recv.at[n], at_lag(lag_near(k))).start()

    def o_sib(n):
        return remote(ob.at[n, :, :, other_lanes], sb.at[n], os_send.at[n], os_recv.at[n], sibling)

    def o_pass(n):
        view = ob.at[n, pl.ds(0, 7)]
        remote(view, view, o_send.at[n], o_recv.at[n], sibling).wait_recv()
        o_sib(n).start()

    def o_finish(n):
        o_sib(n).wait_recv()
        out_ref[n, my_half] = ob[n, :, :, my_lanes].reshape(64, ROWS)
        out_ref[n, other_half] = sb[n].reshape(64, ROWS)

    def products(n, of):
        value = jnp.concatenate(halves(mb[of].reshape(64, BLOCK)), axis=0)
        high, low = halves(w12[n])
        total = lax.dot_general(value, high, NT, preferred_element_type=F32)
        total = total + lax.dot_general(value, low, NT, preferred_element_type=F32)
        return total[0:64] + total[64:128]

    def history_blocks(n, first, last):
        @pl.loop(first, last)
        def _(k):
            block_product(n, k)

    finish_history(0)
    w_pass(0)

    @pl.when(lag != 0)
    def _():
        for batch in older.stage2():
            for copy in batch:
                copy.start()

    c_arrived(0)
    ub[0] = hb[0].reshape(8, 8, BLOCK)
    r_start(0)
    w_pass(1)
    r_sum(0)
    a_start(0)

    @pl.when(lag != 0)
    def _():
        for batch in older.stage3():
            for copy in batch:
                copy.start()
        for i in range(8):
            older.from_sibling(i, *SIB[i])

    inverse(0)
    m_start(0)
    o_start(0)
    history_blocks(1, 0, 8)
    finish_history(1)
    w_sib_arrived(0)
    w_sib_arrived(1)
    c_arrived(1)
    m_wait(0)
    ub[1] = (hb[1] + products(0, 0)).reshape(8, 8, BLOCK)
    r_start(1)
    history_blocks(2, 0, 4)
    r_sum(1)
    a_start(1)
    history_blocks(2, 4, 8)
    finish_history(2)
    inverse(1)
    m_start(1)
    o_start(1)
    c_arrived(2)
    later = hb[2] + products(1, 0)
    o_pass(0)
    m_wait(1)
    ub[2] = (later + products(0, 1)).reshape(8, 8, BLOCK)
    r_start(2)
    o_finish(0)
    o_pass(1)
    r_sum(2)
    a_start(2)
    o_finish(1)
    inverse(2)
    o_start(2)
    o_pass(2)

    for copy in past.everything():
        copy.wait_send()

    @pl.when(lag != 0)
    def _():
        for copy in older.everything():
            copy.wait_send()

    @pl.when(lag < 7)
    def _():
        handed.wait_send()

    @pl.when(lag == 0)
    def _():
        for n in range(2):
            view = w_hbm.at[n, :, pl.ds(0, 7 * BLOCK)]
            pltpu.make_async_copy(view, view, w_send.at[n]).wait()

    for n in range(2):
        w_sib(n).wait_send()
    for n in range(STEPS):
        c_copy(n).wait_send()
        view = rb.at[n]
        remote(view, view, r_send.at[n], r_recv.at[n], sibling).wait_send()
        view = ab.at[n, pl.ds(0, 7)]
        remote(view, view, a_send.at[n], a_recv.at[n, 0], sibling).wait_send()
        view = ob.at[n, pl.ds(0, 7)]
        remote(view, view, o_send.at[n], o_recv.at[n], sibling).wait_send()
        o_sib(n).wait_send()
    o_finish(2)


def on_device(lag_weights, inverse_head, excitation, history):
    vmem = pltpu.VMEM
    dma = pltpu.SemaphoreType.DMA
    turned = pl.pallas_call(
        kernel,
        out_shape=jax.ShapeDtypeStruct((STEPS, EXC, ROWS), F32),
        in_specs=[pl.BlockSpec(memory_space=pl.ANY)] * 4,
        out_specs=pl.BlockSpec(memory_space=pltpu.VMEM),
        scratch_shapes=[
            vmem((LAGS, ROWS, M), F32),
            vmem((LAGS + 2, M, EXC), F32),
            vmem((ROWS, M), F32),
            vmem((ROWS, M), F32),
            vmem((M, BLOCK), BF16),
            vmem((M, BLOCK), BF16),
            vmem((2, BLOCK, BLOCK), F32),
            vmem((STEPS, ROWS, EXC), F32),
            vmem((STEPS, ROWS, 2 * EXC), F32),
            vmem((STEPS, EXC, ROWS), F32),
            vmem((STEPS, 64, BLOCK), F32),
            vmem((STEPS, 8, 8, BLOCK), F32),
            vmem((STEPS, 7, 8, BLOCK), F32),
            vmem((STEPS, 8, 8, BLOCK), F32),
            vmem((STEPS, 8, BLOCK), F32),
            vmem((2, 8, 8, BLOCK), F32),
            vmem((STEPS, 8, 8, BLOCK), F32),
            vmem((STEPS, 8, 8, ROWS), F32),
            dma((6,)),
            dma((12,)), dma((12,)), dma((8,)), dma((8,)),
            dma((12,)), dma((12,)), dma((8,)), dma((8,)),
            dma((4,)), dma((4,)), dma((2,)), dma((2,)),
            dma((STEPS,)), dma((STEPS,)), dma((STEPS,)), dma((STEPS,)),
            dma((STEPS,)), dma((STEPS, 7)), dma((2,)), dma((2,)),
            dma((STEPS,)), dma((STEPS,)), dma((STEPS,)), dma((STEPS,)),
        ],
        compiler_params=pltpu.CompilerParams(
            collective_id=0, has_side_effects=True, vmem_limit_bytes=58 << 20
        ),
        name="steps",
    )(lag_weights, inverse_head, excitation, history)
    return jnp.swapaxes(turned, 1, 2)


def solution(mesh):
    placed = (P("lag", "row", None), P("row", None), P(None, "row", None), P("lag", "row", None))
    return jax.shard_map(
        on_device, mesh=mesh, in_specs=placed, out_specs=P(None, "row", None), check_vma=False
    )
```

time: 454 us -> 197 us (0.43); the launches traced: 447 us -> 197 us
  Pallas kernels: 0 us -> 195 us
  waiting for transfers between devices: 174 us -> 0 us
  blocking collectives: 160 us -> 0 us
  matrix products: 70.6 us -> 0 us
  between operations: 13.5 us -> 0.01 us
  local copies, waits for them, and re-layouts: 12.7 us -> 1.91 us
  other arithmetic: 9.11 us -> 0 us
  starting transfers between devices: 6.42 us -> 0 us
    pallas_call x0 -> x1, Pallas kernels: none -> 195 us  [on_device(): pl.pallas_call(kernel, out_shape=jax.ShapeDtypeStruct((STEPS, EXC, ROWS),...]
    all_to_all x6 -> x0, blocking collectives: 160 us -> none  [sent_to_all(): lax.all_to_all(jnp.broadcast_to(shard[None], (devices, *shard.shape)), ax...]
    ppermute x2 -> x0, waiting for transfers between devices: 94.3 us -> none  [from_behind(): lax.ppermute(value, axis, [(source, source + steps) for source in range(l...]
    all_gather x3 -> x0, waiting for transfers between devices: 79.4 us -> none  [the longest x1 79.4 us: on_device(): past = lax.all_gather(history, 'row', axis=1, tiled=True)]
    dot_general x6 -> x0, matrix products: 70.6 us -> none  [the longest x3 58.9 us: lag_products(): jnp.einsum('kmc,kcr->mr', weights, piece, precision=lax.Precision.HIGHEST)]
    broadcast_in_dim x5 -> x0, other arithmetic: 8.16 us -> none  [the longest x2 4.94 us: on_device(): past = jnp.concatenate([entering[None], past[:-1]], axis=0)]
    ppermute x2 -> x0, starting transfers between devices: 6.33 us -> none  [from_behind(): lax.ppermute(value, axis, [(source, source + steps) for source in range(l...]
    slice x1 -> x0, local copies, waits for them, and re-layouts: 5.89 us -> none  [on_device(): past = jnp.concatenate([entering[None], past[:-1]], axis=0)]
  transfers between devices with their start and end apart: 5 -> 0, of which waited for: 3 -> 0; matrix products, arithmetic and copies ran while one was open for 2% -> 0% of each run, Pallas kernels for 0% -> 0%
where the time goes in v1:
time: 197 us
  Pallas kernels  195 us (99%)
    pallas_call x1, Pallas kernels, on_device(): pl.pallas_call(kernel, out_shape=jax.ShapeDtypeStruct((STEPS, EXC, ROWS),...  195 us

profile of v1, /device:TPU:1, one launch (start us, length us, event | category | flops | bytes accessed | tf_op | source)
XLA Modules:
  0.0 197.0 jit_solution(13616237505168611216)
XLA Ops:
  0.0 195.1 %steps.1 = f32[3,128,256]{2,1,0:T(8,128)} custom-call(f32[4,256,4096]{2,1,0:T(8,128)} %w_hbm.1, f32[256,4096]{1,0:T(8,128)} %h_hbm.1, f32[3,256,128]{2,1,0:T(8,128)} %x_hbm.1, f32[4,256,128]{2,1,0:T(8,128)} %p_hbm.1), custom_call_target="tpu_custom_call" | custom-call | tf_op jit(solution)/shard_map/steps/pallas_call | solution.py:513
  195.1 1.9 copy.5

commit v2 on v1

v2 whole, which is shorter than its diff:
```python
import jax
import jax.numpy as jnp
from jax import lax
from jax.experimental import pallas as pl
from jax.experimental.pallas import tpu as pltpu
from jax.sharding import PartitionSpec as P

STEPS = 3
LAGS = 4
ROWS = 256
M = 4096
EXC = 128
BLOCK = 512
F32 = jnp.float32
BF16 = jnp.bfloat16
MESH = pl.DeviceIdType.MESH
NT = (((1,), (1,)), ((), ()))
NEAR = ((0, 0), (0, 1), (0, 3), (1, 0), (0, 2), (1, 1), (1, 3), (1, 2))


def halves(value):
    high = value.astype(BF16)
    return high, (value - high.astype(F32)).astype(BF16)


def kernel(
    w_hbm, h_hbm, x_hbm, p_hbm, out_ref,
    wv, pg, h_own, h_sib, ht_hi, ht_lo, w12, xv, acc,
    ct, hb, ub, rb, r0, ab, db, mb,
    local_sem, p_send, p_recv, s_send, s_recv, n_send, n_recv, ns_send, ns_recv,
    e_send, e_recv, es_send, es_recv,
    w_send, w_recv, in_send, in_recv, c_send, c_recv, r_send, r_recv,
    a_send, a_recv, m_send, m_recv, o_send, o_recv,
):
    lag = lax.axis_index("lag")
    row = lax.axis_index("row")
    chip, core = row // 2, row % 2
    y, x_lo = lag // 2, lag % 2
    x_hi, z = chip // 4, chip % 4

    def near(dx, dz):
        return ((x_hi + dx) % 2) * 4 + (z + dz) % 4

    def at_chip(other):
        return (lag, other * 2 + core)

    def lag_near(k):
        return ((y + k // 2) % 4) * 2 + (x_lo + k % 2) % 2

    def at_lag(other):
        return (other, row)

    sibling = (lag, chip * 2 + 1 - core)

    def rows_of(a_chip, a_core):
        return pl.ds(pl.multiple_of((a_chip * 2 + a_core) * ROWS, ROWS), ROWS)

    def chip_rows(a_chip):
        return pl.ds(pl.multiple_of(a_chip * BLOCK, BLOCK), BLOCK)

    def remote(src, dst, send, recv, device):
        return pltpu.make_async_remote_copy(
            src_ref=src, dst_ref=dst, send_sem=send, recv_sem=recv,
            device_id=device, device_id_type=MESH,
        )

    def holder_of(a_chip):
        return (a_chip // 4) * (2 + 4 * ((a_chip // 2) % 2))

    holder = holder_of(chip)
    slot = (1 - chip // 4) * chip + (chip // 4) * (chip % 2)
    at_home = lag == holder
    HOLDERS = ((0, 0, 4), (2, 4, 2), (6, 6, 2))

    mine = rows_of(chip, core)
    locals_ = [
        pltpu.make_async_copy(h_hbm, h_own, local_sem.at[0]),
        pltpu.make_async_copy(p_hbm, pg.at[pl.ds(2, LAGS), mine], local_sem.at[1]),
        pltpu.make_async_copy(x_hbm, xv, local_sem.at[2]),
        pltpu.make_async_copy(w_hbm, wv, local_sem.at[3]),
    ]
    for copy in locals_:
        copy.start()

    barrier = pltpu.get_barrier_semaphore()

    def greet(device):
        pl.semaphore_signal(barrier, inc=1, device_id=device, device_id_type=MESH)

    greet(sibling)
    for k in range(1, 8):
        greet(at_chip(near(k // 4, k % 4)))
        greet(at_lag(lag_near(k)))
        greet((lag_near(k), chip * 2 + 1 - core))
    for who, first, count in HOLDERS:

        @pl.when(lag == who)
        def _():
            for source in range(first, first + count):
                for other in range(8):
                    if other == who:

                        @pl.when(chip != source)
                        def _():
                            greet((other, source * 2 + core))
                    else:
                        greet((other, source * 2 + core))

    @pl.when(at_home)
    def _():
        pl.semaphore_wait(barrier, 29)

    @pl.when(jnp.logical_not(at_home))
    def _():
        pl.semaphore_wait(barrier, 30)

    up, down, across = at_chip(near(0, 1)), at_chip(near(0, 3)), at_chip(near(1, 0))

    class Gather:
        def __init__(self, first, count, send, recv, ssend, srecv):
            self.first, self.count = first, count
            self.send, self.recv, self.ssend, self.srecv = send, recv, ssend, srecv
            self.all = (first, count, 0, ROWS)
            if count == LAGS:
                self.low, self.high = (first, 2, 0, ROWS), (first + 2, 2, 0, ROWS)
                self.b1, self.b2 = (first + 2, 1, 0, ROWS), (first + 3, 1, 0, ROWS)
            else:
                self.low, self.high = (first, 1, 0, 128), (first, 1, 128, 128)
                self.b1, self.b2 = (first, 1, 128, 64), (first, 1, 192, 64)

        def view(self, dx, dz, part, a_core=None):
            start, count, offset, size = part
            base = (near(dx, dz) * 2 + (core if a_core is None else a_core)) * ROWS + offset
            return pg.at[pl.ds(start, count), pl.ds(pl.multiple_of(base, 64), size)]

        def copy(self, index, dx, dz, part, device, src=None):
            view = self.view(dx, dz, part)
            return remote(view if src is None else src, view, self.send.at[index], self.recv.at[index], device)

        def arrived(self, index, dx, dz, part):
            view = self.view(dx, dz, part)
            remote(view, view, self.send.at[index], self.recv.at[index], up).wait_recv()

        def to_sibling(self, dx, dz, src=None):
            index = dx * 4 + dz
            view = self.view(dx, dz, self.all)
            return remote(view if src is None else src, view, self.ssend.at[index], self.srecv.at[index], sibling)

        def from_sibling(self, index):
            view = self.view(index // 4, index % 4, self.all, 1 - core)
            remote(view, view, self.ssend.at[index], self.srecv.at[index], sibling).wait_recv()

        def start(self, src=None):
            return [
                self.copy(0, 0, 0, self.all, up, src),
                self.copy(1, 0, 0, self.all, down, src),
                self.copy(2, 0, 0, self.all, across, src),
                self.to_sibling(0, 0, src),
            ]

        def stage1(self):
            self.arrived(0, 0, 3, self.all)
            out = [self.copy(3, 0, 3, self.low, up), self.copy(5, 0, 3, self.low, across), self.to_sibling(0, 3)]
            yield out
            self.arrived(1, 0, 1, self.all)
            out = [self.copy(4, 0, 1, self.high, down), self.copy(6, 0, 1, self.low, across), self.to_sibling(0, 1)]
            yield out
            self.arrived(2, 1, 0, self.all)
            yield [self.copy(8, 1, 0, self.high, up), self.copy(9, 1, 0, self.high, down), self.to_sibling(1, 0)]

        def stage2(self):
            self.arrived(3, 0, 2, self.low)
            yield [self.copy(7, 0, 2, self.low, across)]
            self.arrived(4, 0, 2, self.high)
            yield [self.to_sibling(0, 2)]
            self.arrived(8, 1, 3, self.high)
            yield [self.copy(10, 1, 3, self.b1, up)]
            self.arrived(9, 1, 1, self.high)
            yield [self.copy(11, 1, 1, self.b2, down)]
            self.arrived(5, 1, 3, self.low)
            yield [self.to_sibling(1, 3)]
            self.arrived(6, 1, 1, self.low)
            yield [self.to_sibling(1, 1)]

        def stage3(self):
            self.arrived(7, 1, 2, self.low)
            self.arrived(10, 1, 2, self.b1)
            self.arrived(11, 1, 2, self.b2)
            yield [self.to_sibling(1, 2)]

        def everything(self):
            return (
                [self.copy(i, 0, 0, self.all, up) for i in range(3)]
                + [self.copy(i, 0, 0, self.low, up) for i in range(3, 10)]
                + [self.copy(i, 0, 0, self.b1, up) for i in (10, 11)]
                + [self.to_sibling(i // 4, i % 4) for i in range(8)]
            )

    def place(i):
        close = 2 * i - i // 3 - (i + 7) // 8
        far = 3 * i - 10 - i // 6 - 4 * (i // 7)
        return (1 - i // 4) * close + (i // 4) * far

    past = Gather(2, LAGS, p_send, p_recv, s_send, s_recv)
    newer = Gather(1, 1, n_send, n_recv, ns_send, ns_recv)
    older = Gather(0, 1, e_send, e_recv, es_send, es_recv)

    for copy in past.start(p_hbm):
        copy.start()
    to_h = remote(h_hbm, h_sib, in_send.at[0], in_recv.at[0], sibling)
    to_h.start()

    e_view = pg.at[pl.ds(0, 2), mine]
    next_group = ((lag + 1) % 8, row)
    handed = remote(p_hbm.at[pl.ds(2, 2)], e_view, in_send.at[1], in_recv.at[1], next_group)

    def w_half(n, half):
        return w12.at[n, :, pl.ds(pl.multiple_of(half * 2 * BLOCK, 2 * BLOCK), 2 * BLOCK)]

    def w_from(n, first, count):
        return w_hbm.at[n, :, pl.ds(first * BLOCK, count * BLOCK)]

    def w_copy(n, who, first, count):
        return remote(w_from(n, first, count), w_half(n, core), w_send.at[n], w_recv.at[n], (who, row))

    def w_sib(n, who):
        src, dst = (w_from(n, 0, 4), w12.at[n]) if who == 0 else (w_half(n, core), w_half(n, core))
        return remote(src, dst, w_send.at[2 + n], w_recv.at[2 + n], sibling)

    def w_start(n):
        @pl.when(lag == 0)
        def _():
            for held in HOLDERS[1:]:
                w_copy(n, *held).start()
            w_sib(n, 0).start()

    def w_pass(n):
        for who, first, count in HOLDERS[1:]:

            @pl.when(lag == who)
            def _():
                w_copy(n, who, first, count).wait_recv()
                w_sib(n, who).start()

    def w_wait(n):
        for who, _, _ in HOLDERS:

            @pl.when(lag == who)
            def _():
                w_sib(n, who).wait_recv()

    w_start(0)
    w_start(1)

    @pl.when(lag < 7)
    def _():
        handed.start()

    @pl.when(lag == 0)
    def _():
        pg[0:2] = jnp.zeros((2, M, EXC), F32)

    def block_product(n, a_chip, first=0, last=LAGS):
        rows = chip_rows(a_chip)
        values, highs, lows = [], [], []
        for i in range(first, last):
            values.append(jnp.concatenate(halves(pg[2 + i - n, rows, :]), axis=1))
            high, low = halves(wv[i, :, rows])
            highs.append(high)
            lows.append(low)
        value = jnp.concatenate(values, axis=0)
        acc[n] += jnp.dot(jnp.concatenate(highs, axis=1), value, preferred_element_type=F32) + jnp.dot(
            jnp.concatenate(lows, axis=1), value, preferred_element_type=F32
        )

    acc[...] = jnp.zeros(acc.shape, F32)

    locals_[0].wait()

    def turn(source, half):
        @pl.loop(0, 8)
        def _(k):
            rows = pl.ds(pl.multiple_of(k * BLOCK, BLOCK), BLOCK)
            lanes = pl.ds(pl.multiple_of(half * ROWS, ROWS), ROWS)
            high, low = halves(source[:, rows].T)
            ht_hi[rows, lanes] = high
            ht_lo[rows, lanes] = low

    turn(h_own, core)
    to_h.wait()
    turn(h_sib, 1 - core)
    locals_[1].wait()
    locals_[3].wait()

    def run(copies):
        for batch in copies:
            for copy in batch:
                copy.start()

    def outer(copies):
        @pl.when(lag != 0)
        def _():
            run(copies())

    locals_[2].wait()

    @pl.loop(0, 8)
    def _(i):
        @pl.when(i == 1)
        def _():
            run(past.stage1())

        @pl.when(i == 4)
        def _():
            run(past.stage2())

            @pl.when(lag != 0)
            def _():
                remote(e_view, e_view, in_send.at[1], in_recv.at[1], next_group).wait_recv()
                run([newer.start()])

        @pl.when(i == 7)
        def _():
            run(past.stage3())
            outer(newer.stage1)

        k = place(i)
        past.from_sibling(k)
        block_product(0, near(k // 4, k % 4))

    owner = lax.broadcasted_iota(jnp.int32, (EXC, ROWS), 0) % 64 // 8
    my_half = pl.ds(pl.multiple_of(core * 64, 64), 64)
    other_half = pl.ds(pl.multiple_of((1 - core) * 64, 64), 64)
    my_lanes = pl.ds(pl.multiple_of(core * ROWS, ROWS), ROWS)
    other_lanes = pl.ds(pl.multiple_of((1 - core) * ROWS, ROWS), ROWS)

    def c_copy(n):
        return remote(ct.at[n, other_half], hb.at[n, :, my_lanes], c_send.at[n], c_recv.at[n], sibling)

    def c_arrived(n):
        view = hb.at[n, :, other_lanes]
        remote(view, view, c_send.at[n], c_recv.at[n], sibling).wait_recv()

    def turn_history(n):
        total = (acc[n, :, 0:EXC] + acc[n, :, EXC:]).T
        ct[n] = total - jnp.where(owner == lag, xv[n].T, 0.0)

    def finish_history(n):
        turn_history(n)
        c_copy(n).start()
        hb[n, :, my_lanes] = ct[n, my_half]

    def eight(a_core, a_lag):
        return pl.ds(pl.multiple_of(a_core * 64 + a_lag * 8, 8), 8)

    def r_first():
        for k in range(8):
            for other_core in (1 - core, core) if k else (1 - core,):
                other = lag_near(k)
                remote(
                    ct.at[0, eight(other_core, other)], r0.at[k, :, my_lanes],
                    r_send.at[0], r_recv.at[0 if k else STEPS], (other, chip * 2 + other_core),
                ).start()
        r0[0, :, my_lanes] = ct[0, eight(core, lag)]

    def r_first_sum():
        view = r0.at[pl.ds(1, 7)]
        remote(view, view, r_send.at[0], r_recv.at[0], sibling).wait_recv()
        view = r0.at[0, :, other_lanes]
        remote(view, view, r_send.at[0], r_recv.at[STEPS], sibling).wait_recv()
        total = r0[0]
        for k in range(1, 8):
            total = total + r0[k]
        ab[0, chip] = -total

    def r_start(n):
        for k in range(1, 8):
            other = lag_near(k)
            remote(ub.at[n, other], rb.at[n, k - 1], r_send.at[n], r_recv.at[n], at_lag(other)).start()

    def r_sum(n):
        view = rb.at[n]
        remote(view, view, r_send.at[n], r_recv.at[n], sibling).wait_recv()
        total = ub[n, lag]
        for k in range(7):
            total = total + rb[n, k]
        ab[n, chip] = -total

    def a_start(n):
        for dx, dz in NEAR[1:]:
            k = dx * 4 + dz
            remote(
                ab.at[n, chip], ab.at[n, chip], a_send.at[n], a_recv.at[n, k], at_chip(near(dx, dz))
            ).start()

    def inverse(n):
        def pair(j, total):
            for i in (2 * j, 2 * j + 1):
                k = place(i)
                source = near(2 - k // 4, 4 - k % 4)

                @pl.when(k > 0)
                def _():
                    view = ab.at[n, source]
                    remote(view, view, a_send.at[n], a_recv.at[n, k], sibling).wait_recv()

                value = jnp.concatenate(halves(ab[n, source]), axis=0)
                rows = chip_rows(source)
                total = total + jnp.dot(value, ht_hi[rows, :], preferred_element_type=F32)
                total = total + jnp.dot(value, ht_lo[rows, :], preferred_element_type=F32)
            return total

        total = lax.fori_loop(0, 4, pair, jnp.zeros((16, BLOCK), F32))
        db[n] = total[0:8] + total[8:16]

    def m_copy(n, k):
        other = (chip + k) % 8
        return remote(db.at[n], mb.at[n, slot * 8 + lag], m_send.at[n], m_recv.at[n], (holder, other * 2 + core))

    def m_start(n):
        for k in range(1, 8):
            m_copy(n, k).start()

        @pl.when(jnp.logical_not(at_home))
        def _():
            m_copy(n, 0).start()

        @pl.when(at_home)
        def _():
            mb[n, slot * 8 + lag] = db[n]

    def m_wait(n):
        def some(count):
            view = mb.at[n, pl.ds(0, count)]
            remote(view, view, m_send.at[n], m_recv.at[n], sibling).wait_recv()

        for who, _, count in HOLDERS:

            @pl.when(jnp.logical_and(lag == who, at_home))
            def _():
                some(count * 8 - 1)

            @pl.when(jnp.logical_and(lag == who, jnp.logical_not(at_home)))
            def _():
                some(count * 8)

    def m_sent(n):
        def some(count):
            view = mb.at[n, pl.ds(0, count)]
            remote(view, view, m_send.at[n], m_recv.at[n], sibling).wait_send()

        @pl.when(at_home)
        def _():
            some(7)

        @pl.when(jnp.logical_not(at_home))
        def _():
            some(8)

    def o_start(n):
        spot = eight(core, lag)
        for k in range(8):
            for other_core in (1 - core, core) if k else (1 - core,):
                lanes = pl.ds(pl.multiple_of(other_core * ROWS, ROWS), ROWS)
                remote(
                    db.at[n, :, lanes], out_ref.at[n, spot],
                    o_send.at[n], o_recv.at[n], (lag_near(k), chip * 2 + other_core),
                ).start()
        out_ref[n, spot] = db[n, :, my_lanes]

    def o_done(n):
        view = out_ref.at[n, pl.ds(0, 120)]
        remote(view, view, o_send.at[n], o_recv.at[n], sibling).wait()

    def add_products(n, of):
        def add(ref, start, part, lanes):
            values = mb[of, pl.ds(part * 8, 8)].reshape(64, BLOCK)
            value = jnp.concatenate(halves(values), axis=0)
            high, low = halves(ref[n, :, pl.ds(pl.multiple_of(start, BLOCK), BLOCK)])
            total = lax.dot_general(value, high, NT, preferred_element_type=F32)
            total = total + lax.dot_general(value, low, NT, preferred_element_type=F32)
            hb[n + of + 1, :, lanes] += total[0:64] + total[64:128]

        @pl.when(lag == 0)
        def _():
            @pl.loop(0, 4)
            def _(part):
                add(wv, part * BLOCK, part, my_lanes)
                add(w12, part * BLOCK, part, other_lanes)

        @pl.when(jnp.logical_or(lag == 2, lag == 6))
        def _():
            @pl.loop(0, 2)
            def _(part):
                add(w12, (core * 2 + part) * BLOCK, part, my_lanes)
                add(w12, (2 - core * 2 + part) * BLOCK, part, other_lanes)

    def history_blocks(n, first, last, lags):
        @pl.loop(first, last)
        def _(k):
            block_product(n, k, *lags)

    def whole(gather):
        @pl.when(lag != 0)
        def _():
            for i in range(8):
                gather.from_sibling(i)

    turn_history(0)
    r_first()
    history_blocks(1, 0, 4, (1, 4))
    r_first_sum()
    a_start(0)
    outer(newer.stage2)
    history_blocks(1, 4, 8, (1, 4))
    w_pass(0)
    inverse(0)
    m_start(0)
    o_start(0)
    outer(newer.stage3)
    outer(lambda: [older.start()])
    history_blocks(2, 0, 8, (2, 4))
    whole(newer)
    history_blocks(1, 0, 8, (0, 1))
    finish_history(1)
    w_wait(0)
    outer(older.stage1)
    m_wait(0)
    c_arrived(1)
    add_products(0, 0)
    ub[1] = hb[1].reshape(8, 8, BLOCK)
    r_start(1)
    w_pass(1)
    r_sum(1)
    a_start(1)
    outer(older.stage2)
    inverse(1)
    m_start(1)
    o_start(1)
    outer(older.stage3)
    whole(older)
    history_blocks(2, 0, 8, (0, 2))
    finish_history(2)
    c_arrived(2)
    w_wait(1)
    add_products(1, 0)
    m_wait(1)
    add_products(0, 1)
    ub[2] = hb[2].reshape(8, 8, BLOCK)
    r_start(2)
    o_done(0)
    r_sum(2)
    a_start(2)
    o_done(1)
    inverse(2)
    o_start(2)

    for copy in past.everything():
        copy.wait_send()

    @pl.when(lag != 0)
    def _():
        for copy in newer.everything() + older.everything():
            copy.wait_send()

    @pl.when(lag < 7)
    def _():
        handed.wait_send()

    for n in range(2):
        m_sent(n)

        @pl.when(lag == 0)
        def _():
            view = w_from(n, 4, 4)
            pltpu.make_async_copy(view, view, w_send.at[n]).wait()

        for who, _, _ in HOLDERS:

            @pl.when(lag == who)
            def _():
                w_sib(n, who).wait_send()

    view = ct.at[0, pl.ds(0, 120)]
    remote(view, view, r_send.at[0], r_recv.at[0], sibling).wait_send()
    for n in range(STEPS):
        if n > 0:
            c_copy(n).wait_send()
            view = rb.at[n]
            remote(view, view, r_send.at[n], r_recv.at[n], sibling).wait_send()
        view = ab.at[n, pl.ds(0, 7)]
        remote(view, view, a_send.at[n], a_recv.at[n, 1], sibling).wait_send()
    o_done(2)


def on_device(lag_weights, inverse_head, excitation, history):
    vmem = pltpu.VMEM
    dma = pltpu.SemaphoreType.DMA
    turned = pl.pallas_call(
        kernel,
        out_shape=jax.ShapeDtypeStruct((STEPS, EXC, ROWS), F32),
        in_specs=[pl.BlockSpec(memory_space=pl.ANY)] * 4,
        out_specs=pl.BlockSpec(memory_space=pltpu.VMEM),
        scratch_shapes=[
            vmem((LAGS, ROWS, M), F32),
            vmem((LAGS + 2, M, EXC), F32),
            vmem((ROWS, M), F32),
            vmem((ROWS, M), F32),
            vmem((M, BLOCK), BF16),
            vmem((M, BLOCK), BF16),
            vmem((2, ROWS, 4 * BLOCK), F32),
            vmem((STEPS, ROWS, EXC), F32),
            vmem((STEPS, ROWS, 2 * EXC), F32),
            vmem((STEPS, EXC, ROWS), F32),
            vmem((STEPS, 64, BLOCK), F32),
            vmem((STEPS, 8, 8, BLOCK), F32),
            vmem((STEPS, 7, 8, BLOCK), F32),
            vmem((8, 8, BLOCK), F32),
            vmem((STEPS, 8, 8, BLOCK), F32),
            vmem((STEPS, 8, BLOCK), F32),
            vmem((2, 32, 8, BLOCK), F32),
            dma((6,)),
            dma((12,)), dma((12,)), dma((8,)), dma((8,)),
            dma((12,)), dma((12,)), dma((8,)), dma((8,)),
            dma((12,)), dma((12,)), dma((8,)), dma((8,)),
            dma((4,)), dma((4,)), dma((2,)), dma((2,)),
            dma((STEPS,)), dma((STEPS,)), dma((STEPS,)), dma((STEPS + 1,)),
            dma((STEPS,)), dma((STEPS, 8)), dma((2,)), dma((2,)),
            dma((STEPS,)), dma((STEPS,)),
        ],
        compiler_params=pltpu.CompilerParams(
            collective_id=0, has_side_effects=True, vmem_limit_bytes=58 << 20
        ),
        name="steps",
    )(lag_weights, inverse_head, excitation, history)
    return jnp.swapaxes(turned, 1, 2)


def solution(mesh):
    placed = (P("lag", "row", None), P("row", None), P(None, "row", None), P("lag", "row", None))
    return jax.shard_map(
        on_device, mesh=mesh, in_specs=placed, out_specs=P(None, "row", None), check_vma=False
    )
```

time: 197 us -> 118 us (0.60)
  Pallas kernels: 195 us -> 116 us
    pallas_call x1, Pallas kernels: 195 us -> 116 us  [on_device(): pl.pallas_call(kernel, out_shape=jax.ShapeDtypeStruct((STEPS, EXC, ROWS),...]
where the time goes in v2:
time: 118 us
  Pallas kernels  116 us (98%)
  local copies, waits for them, and re-layouts  1.91 us (2%)
    pallas_call x1, Pallas kernels, on_device(): pl.pallas_call(kernel, out_shape=jax.ShapeDtypeStruct((STEPS, EXC, ROWS),...  116 us

profile of v2, /device:TPU:1, one launch (start us, length us, event | category | flops | bytes accessed | tf_op | source)
XLA Modules:
  0.0 118.0 jit_solution(5741575414183785888)
XLA Ops:
  0.0 116.1 %steps.1 = f32[3,128,256]{2,1,0:T(8,128)} custom-call(f32[4,256,4096]{2,1,0:T(8,128)} %w_hbm.1, f32[256,4096]{1,0:T(8,128)} %h_hbm.1, f32[3,256,128]{2,1,0:T(8,128)} %x_hbm.1, f32[4,256,128]{2,1,0:T(8,128)} %p_hbm.1), custom_call_target="tpu_custom_call" | custom-call | tf_op jit(solution)/shard_map/steps/pallas_call | solution.py:599
  116.1 1.9 %copy.5 = f32[3,256,128]{2,1,0:T(8,128)} copy(f32[3,256,128]{1,2,0:T(8,128)} %bitcast.1) | data formatting | bytes 786432 | tf_op jit(solution)/shard_map/transpose | solution.py:636

commit v3 on v2

--- a/solution.py
+++ b/solution.py
@@ -204,6 +204,8 @@
     past = Gather(2, LAGS, p_send, p_recv, s_send, s_recv)
     newer = Gather(1, 1, n_send, n_recv, ns_send, ns_recv)
     older = Gather(0, 1, e_send, e_recv, es_send, es_recv)
+    fresh = Gather(LAGS + 2, 1, n_send, n_recv, ns_send, ns_recv)
+    before = 1 + 5 * (lag == 0).astype(jnp.int32)
 
     for copy in past.start(p_hbm):
         copy.start()
@@ -250,7 +252,6 @@
                 w_sib(n, who).wait_recv()
 
     w_start(0)
-    w_start(1)
 
     @pl.when(lag < 7)
     def _():
@@ -264,7 +265,8 @@
         rows = chip_rows(a_chip)
         values, highs, lows = [], [], []
         for i in range(first, last):
-            values.append(jnp.concatenate(halves(pg[2 + i - n, rows, :]), axis=1))
+            slot = before if (n, i) == (2, 1) else 2 + i - n
+            values.append(jnp.concatenate(halves(pg[slot, rows, :]), axis=1))
             high, low = halves(wv[i, :, rows])
             highs.append(high)
             lows.append(low)
@@ -523,32 +525,49 @@
     whole(newer)
     history_blocks(1, 0, 8, (0, 1))
     finish_history(1)
+    outer(older.stage1)
+    o_done(0)
+
+    def first_only(copies):
+        @pl.when(lag == 0)
+        def _():
+            run(copies())
+
+    @pl.when(lag == 0)
+    def _():
+        pg[LAGS + 2, mine] = out_ref[0].T
+        run([fresh.start()])
+
     w_wait(0)
-    outer(older.stage1)
     m_wait(0)
     c_arrived(1)
     add_products(0, 0)
     ub[1] = hb[1].reshape(8, 8, BLOCK)
     r_start(1)
-    w_pass(1)
+    first_only(fresh.stage1)
     r_sum(1)
     a_start(1)
     outer(older.stage2)
+    first_only(fresh.stage2)
     inverse(1)
     m_start(1)
     o_start(1)
     outer(older.stage3)
     whole(older)
+
+    @pl.when(lag == 0)
+    def _():
+        run(fresh.stage3())
+        for i in range(8):
+            fresh.from_sibling(i)
+
     history_blocks(2, 0, 8, (0, 2))
     finish_history(2)
     c_arrived(2)
-    w_wait(1)
-    add_products(1, 0)
     m_wait(1)
     add_products(0, 1)
     ub[2] = hb[2].reshape(8, 8, BLOCK)
     r_start(2)
-    o_done(0)
     r_sum(2)
     a_start(2)
     o_done(1)
@@ -558,9 +577,12 @@
     for copy in past.everything():
         copy.wait_send()
 
+    for copy in newer.everything():
+        copy.wait_send()
+
     @pl.when(lag != 0)
     def _():
-        for copy in newer.everything() + older.everything():
+        for copy in older.everything():
             copy.wait_send()
 
     @pl.when(lag < 7)
@@ -570,16 +592,16 @@
     for n in range(2):
         m_sent(n)
 
-        @pl.when(lag == 0)
-        def _():
-            view = w_from(n, 4, 4)
-            pltpu.make_async_copy(view, view, w_send.at[n]).wait()
-
-        for who, _, _ in HOLDERS:
-
-            @pl.when(lag == who)
-            def _():
-                w_sib(n, who).wait_send()
+    @pl.when(lag == 0)
+    def _():
+        view = w_from(0, 4, 4)
+        pltpu.make_async_copy(view, view, w_send.at[0]).wait()
+
+    for who, _, _ in HOLDERS:
+
+        @pl.when(lag == who)
+        def _():
+            w_sib(0, who).wait_send()
 
     view = ct.at[0, pl.ds(0, 120)]
     remote(view, view, r_send.at[0], r_recv.at[0], sibling).wait_send()
@@ -603,12 +625,12 @@
         out_specs=pl.BlockSpec(memory_space=pltpu.VMEM),
         scratch_shapes=[
             vmem((LAGS, ROWS, M), F32),
-            vmem((LAGS + 2, M, EXC), F32),
+            vmem((LAGS + 3, M, EXC), F32),
             vmem((ROWS, M), F32),
             vmem((ROWS, M), F32),
             vmem((M, BLOCK), BF16),
             vmem((M, BLOCK), BF16),
-            vmem((2, ROWS, 4 * BLOCK), F32),
+            vmem((1, ROWS, 4 * BLOCK), F32),
             vmem((STEPS, ROWS, EXC), F32),
             vmem((STEPS, ROWS, 2 * EXC), F32),
             vmem((STEPS, EXC, ROWS), F32),

time: 118 us -> 109 us (0.924)
  Pallas kernels: 116 us -> 107 us
    pallas_call x1, Pallas kernels: 116 us -> 107 us  [on_device(): pl.pallas_call(kernel, out_shape=jax.ShapeDtypeStruct((STEPS, EXC, ROWS),...]
where the time goes in v3:
time: 109 us; the launch traced here: 108 us
  Pallas kernels  107 us (98%)
  local copies, waits for them, and re-layouts  1.91 us (2%)
    pallas_call x1, Pallas kernels, on_device(): pl.pallas_call(kernel, out_shape=jax.ShapeDtypeStruct((STEPS, EXC, ROWS),...  107 us

profile of v3, /device:TPU:1, one launch (start us, length us, event | category | flops | bytes accessed | tf_op | source)
XLA Modules:
  0.0 108.5 jit_solution(18132451041801408146)
XLA Ops:
  0.0 106.6 %steps.1 = f32[3,128,256]{2,1,0:T(8,128)} custom-call(f32[4,256,4096]{2,1,0:T(8,128)} %w_hbm.1, f32[256,4096]{1,0:T(8,128)} %h_hbm.1, f32[3,256,128]{2,1,0:T(8,128)} %x_hbm.1, f32[4,256,128]{2,1,0:T(8,128)} %p_hbm.1), custom_call_target="tpu_custom_call" | custom-call | tf_op jit(solution)/shard_map/steps/pallas_call | solution.py:621
  106.6 1.9 %copy.5 = f32[3,256,128]{2,1,0:T(8,128)} copy(f32[3,256,128]{1,2,0:T(8,128)} %bitcast.1) | data formatting | bytes 786432 | tf_op jit(solution)/shard_map/transpose | solution.py:658

commit v4 on v3

--- a/solution.py
+++ b/solution.py
@@ -396,23 +396,17 @@
             ).start()
 
     def inverse(n):
-        def pair(j, total):
-            for i in (2 * j, 2 * j + 1):
-                k = place(i)
-                source = near(2 - k // 4, 4 - k % 4)
-
-                @pl.when(k > 0)
-                def _():
-                    view = ab.at[n, source]
-                    remote(view, view, a_send.at[n], a_recv.at[n, k], sibling).wait_recv()
-
-                value = jnp.concatenate(halves(ab[n, source]), axis=0)
-                rows = chip_rows(source)
-                total = total + jnp.dot(value, ht_hi[rows, :], preferred_element_type=F32)
-                total = total + jnp.dot(value, ht_lo[rows, :], preferred_element_type=F32)
-            return total
-
-        total = lax.fori_loop(0, 4, pair, jnp.zeros((16, BLOCK), F32))
+        total = jnp.zeros((16, BLOCK), F32)
+        for i in range(8):
+            k = place(i)
+            source = near(2 - k // 4, 4 - k % 4)
+            if k > 0:
+                view = ab.at[n, source]
+                remote(view, view, a_send.at[n], a_recv.at[n, k], sibling).wait_recv()
+            value = jnp.concatenate(halves(ab[n, source]), axis=0)
+            rows = chip_rows(source)
+            total = total + jnp.dot(value, ht_hi[rows, :], preferred_element_type=F32)
+            total = total + jnp.dot(value, ht_lo[rows, :], preferred_element_type=F32)
         db[n] = total[0:8] + total[8:16]
 
     def m_copy(n, k):

time: 109 us -> 109 us (level)
  no operation moved by 1% of the time
where the time goes in v4:
time: 109 us
  Pallas kernels  107 us (98%)
  local copies, waits for them, and re-layouts  1.91 us (2%)
    pallas_call x1, Pallas kernels, on_device(): pl.pallas_call(kernel, out_shape=jax.ShapeDtypeStruct((STEPS, EXC, ROWS),...  107 us

profile of v4, /device:TPU:1, one launch (start us, length us, event | category | flops | bytes accessed | tf_op | source)
XLA Modules:
  0.0 108.9 jit_solution(2611112815676461357)
XLA Ops:
  0.0 107.0 %steps.1 = f32[3,128,256]{2,1,0:T(8,128)} custom-call(f32[4,256,4096]{2,1,0:T(8,128)} %w_hbm.1, f32[256,4096]{1,0:T(8,128)} %h_hbm.1, f32[3,256,128]{2,1,0:T(8,128)} %x_hbm.1, f32[4,256,128]{2,1,0:T(8,128)} %p_hbm.1), custom_call_target="tpu_custom_call" | custom-call | tf_op jit(solution)/shard_map/steps/pallas_call | solution.py:615
  107.0 1.9 %copy.5 = f32[3,256,128]{2,1,0:T(8,128)} copy(f32[3,256,128]{1,2,0:T(8,128)} %bitcast.1) | data formatting | bytes 786432 | tf_op jit(solution)/shard_map/transpose | solution.py:652
